TPU v7x, 128 devices: a whole 4x4x4 slice. The times are simulated.
128 devices in a mesh: row: 16 (over y, x), col: 8 (over z, core).
Axes of the slice: x: 4, y: 4, z: 4, core: 2. Of those that a mesh axis runs over, the one named last changes fastest.
Arguments:
- tokens: bfloat16 [1024, 8192], P('col', 'row'), may hold values from -6 to 6
- cotangent: bfloat16 [1024, 8192], P('col', 'row'), may hold values from -1.5 to 1.5
- gate_weight: bfloat16 [8192, 14336], P('row', 'col'), may hold values from -0.0625 to 0.0625
- up_weight: bfloat16 [8192, 14336], P('row', 'col'), may hold values from -0.0625 to 0.0625
- down_weight: bfloat16 [14336, 8192], P('col', 'row'), may hold values from -0.046875 to 0.046875
Outputs:
- layer_output: bfloat16 [1024, 8192], P('col', 'row')
- input_grad: bfloat16 [1024, 8192], P('col', 'row')
- gate_weight_grad: bfloat16 [8192, 14336], P('row', 'col')
- up_weight_grad: bfloat16 [8192, 14336], P('row', 'col')
- down_weight_grad: bfloat16 [14336, 8192], P('col', 'row')
All inputs are finite; a program needn't handle non-finite values.
Results may differ from a plain program's by a relative error of at most 0.0049.
Values may be sent and summed in bfloat16 or wider, within the bound.
No kernel may reach another device: no remote copies, remote signals or barrier semaphores. Data moves between devices by JAX's collectives and lax.ppermute only.
A program may use at most 192 MiB of HBM per device.

v0:
```python
import jax
import jax.numpy as jnp
from jax import lax
from jax.sharding import PartitionSpec as P


def contract_last(left, right):
    return lax.dot_general(
        left, right, (((1,), (1,)), ((), ())), preferred_element_type=jnp.float32
    )


def contract_first(left, right):
    return lax.dot_general(
        left, right, (((0,), (0,)), ((), ())), preferred_element_type=jnp.float32
    )


def local(tokens, cotangent, gate_weight, up_weight, down_weight):
    token_panel = lax.all_gather(tokens, "col", axis=0, tiled=True)
    row_share = token_panel.shape[0] // lax.axis_size("row")
    hidden_width = gate_weight.shape[1]
    partial_sums = jnp.concatenate(
        [
            jnp.dot(token_panel, gate_weight, preferred_element_type=jnp.float32),
            jnp.dot(token_panel, up_weight, preferred_element_type=jnp.float32),
        ],
        axis=1,
    )
    joined = lax.psum(partial_sums, "row")
    gate_all = joined[:, :hidden_width]
    up_all = joined[:, hidden_width:]
    sigmoid_all = jax.nn.sigmoid(gate_all)
    silu_all = gate_all * sigmoid_all
    hidden_panel = (silu_all * up_all).astype(jnp.bfloat16)
    first_own = lax.axis_index("row") * row_share
    own_gate = lax.dynamic_slice_in_dim(gate_all, first_own, row_share, 0)
    own_up = lax.dynamic_slice_in_dim(up_all, first_own, row_share, 0)
    sigmoid_gate = lax.dynamic_slice_in_dim(sigmoid_all, first_own, row_share, 0)
    silu_gate = lax.dynamic_slice_in_dim(silu_all, first_own, row_share, 0)
    rows_in = hidden_panel
    layer_output = lax.psum_scatter(
        jnp.dot(rows_in, down_weight, preferred_element_type=jnp.float32),
        "col",
        scatter_dimension=0,
        tiled=True,
    ).astype(jnp.bfloat16)
    grad_panel = lax.all_gather(cotangent, "col", axis=0, tiled=True)
    rows_in = grad_panel
    hidden_grad = lax.psum_scatter(
        contract_last(rows_in, down_weight), "row", scatter_dimension=0, tiled=True
    )
    down_weight_grad = contract_first(hidden_panel, grad_panel).astype(jnp.bfloat16)
    silu_slope = sigmoid_gate * (1.0 + own_gate * (1.0 - sigmoid_gate))
    gate_grad = (hidden_grad * own_up * silu_slope).astype(jnp.bfloat16)
    up_grad = (hidden_grad * silu_gate).astype(jnp.bfloat16)
    gate_grad_panel, up_grad_panel = (
        lax.all_gather(gate_grad, "row", axis=0, tiled=True),
        lax.all_gather(up_grad, "row", axis=0, tiled=True),
    )
    input_grad = lax.psum_scatter(
        contract_last(gate_grad_panel, gate_weight) + contract_last(up_grad_panel, up_weight),
        "col",
        scatter_dimension=0,
        tiled=True,
    ).astype(jnp.bfloat16)
    gate_weight_grad = contract_first(token_panel, gate_grad_panel).astype(jnp.bfloat16)
    up_weight_grad = contract_first(token_panel, up_grad_panel).astype(jnp.bfloat16)
    return (layer_output, input_grad, gate_weight_grad, up_weight_grad, down_weight_grad)


def solution(mesh):
    in_specs = (P("col", "row"), P("col", "row"), P("row", "col"), P("row", "col"), P("col", "row"))
    out_specs = (
        P("col", "row"),
        P("col", "row"),
        P("row", "col"),
        P("row", "col"),
        P("col", "row"),
    )
    return jax.shard_map(local, mesh=mesh, in_specs=in_specs, out_specs=out_specs, check_vma=False)
```

profile of v0, /device:TPU:0, one launch (start us, length us, event | category | flops | bytes accessed | tf_op | source)
XLA Modules:
  0.0 531.8 jit_solution(439490304801279585)
XLA Ops:
  7.2 0.0 copy-start
  7.2 0.0 all-gather.5.cloned.1.call-start
  7.2 0.7 all-gather.5.cloned.1.call-update
  7.9 0.0 all-gather.7.cloned.1.call-start
  8.0 0.7 all-gather.7.cloned.1.call-update
  8.7 0.0 all-reduce.2.cloned.1.call-start
  8.7 27.0 %all-gather.5.cloned.1.call-done = bf16[1024,512]{1,0:T(8,128)(2,1)} async-done(((bf16[128,512]{1,0:T(8,128)(2,1)}), bf16[1024,512]{1,0:T(8,128)(2,1)}) %all-gather.5.cloned.1.call-update) | async-done | bytes 1048592 | tf_op jit(solution)/shard_map/all_gather | solution.py:20
  35.7 0.0 copy-start.1
  35.7 0.0 copy-start.2
  35.7 4.0 fusion.2
  39.7 0.0 copy-done.1
  39.7 0.0 copy-done.2
  39.7 2.1 fusion.3
  41.8 5.8 %pad_maximum_fusion = f32[1024,3584]{1,0:T(8,128)} fusion(f32[1024,1792]{1,0:T(8,128)S(1)} %fusion.3, f32[1024,1792]{1,0:T(8,128)S(1)} %fusion.2), kind=kLoop, calls=%fused_computation | loop fusion | flops 3670016 | bytes 29360128 | tf_op jit(solution)/shard_map/concatenate | solution.py:23
  47.7 0.0 all-reduce.2.cloned.1.call-update
  47.7 0.0 reduce-scatter.6.cloned.1.call-start
  47.7 13.1 %all-gather.7.cloned.1.call-done = bf16[1024,512]{1,0:T(8,128)(2,1)} async-done(((bf16[128,512]{1,0:T(8,128)(2,1)}), bf16[1024,512]{1,0:T(8,128)(2,1)}) %all-gather.7.cloned.1.call-update) | async-done | bytes 1048592 | tf_op jit(solution)/shard_map/all_gather | solution.py:48
  60.8 0.0 copy-done
  60.8 6.3 %fusion.5 = f32[1024,1792]{1,0:T(8,128)} fusion(bf16[1024,512]{1,0:T(8,128)(2,1)} %all-gather.7.cloned.1.call-done, bf16[1792,512]{1,0:T(8,128)(2,1)S(1)} %copy-done), kind=kOutput, calls=%fused_computation.15 | convolution fusion | flops 1879048192 | bytes 10223616 | tf_op jit(solution)/shard_map/dot_general | solution.py:8
  67.1 0.0 reduce-scatter.6.cloned.1.call-update
  67.1 0.0 all-gather.9.cloned.1.call-start
  67.2 195.9 %all-reduce.2.cloned.1.call-done = f32[1024,3584]{1,0:T(8,128)} async-done(((f32[1024,3584]{1,0:T(8,128)}), f32[1024,3584]{1,0:T(8,128)}) %all-reduce.2.cloned.1.call-update) | async-done | bytes 14680080 | tf_op jit(solution)/shard_map/psum | solution.py:30
  263.1 15.5 %slice_multiply_fusion = (f32[1024,1792]{1,0:T(8,128)}, f32[1024,1792]{1,0:T(8,128)}, bf16[1024,1792]{1,0:T(8,128)(2,1)}, f32[1024,1792]{1,0:T(8,128)}, f32[1024,1792]{1,0:T(8,128)}) fusion(f32[1024,3584]{1,0:T(8,128)} %all-reduce.2.cloned.1.call-done), kind=kLoop, calls=%fused_computation.11 | loop fusion | flops 11010048 | bytes 47710208 | tf_op jit(solution)/shard_map/mul | solution.py:34
  278.5 71.4 %reduce-scatter.6.cloned.1.call-done = f32[64,1792]{1,0:T(8,128)} async-done(((f32[1024,1792]{1,0:T(8,128)}), f32[64,1792]{1,0:T(8,128)}) %reduce-scatter.6.cloned.1.call-update) | async-done | bytes 458768 | tf_op jit(solution)/shard_map/reduce_scatter | solution.py:50
  349.9 2.5 multiply_convert_fusion.1
  352.4 0.0 all-gather.9.cloned.1.call-update
  352.4 0.0 all-gather.11.cloned.1.call-start
  352.4 0.5 all-gather.11.cloned.1.call-update
  353.0 0.0 reduce-scatter.4.cloned.1.call-start
  353.0 5.5 %fusion.4 = f32[1024,512]{1,0:T(8,128)} fusion(bf16[1024,1792]{1,0:T(8,128)(2,1)} %get-tuple-element.12, bf16[1792,512]{1,0:T(8,128)(2,1)S(1)} %copy-done), kind=kOutput, calls=%fused_computation.14 | convolution fusion | flops 1879048192 | bytes 7602176 | tf_op jit(solution)/shard_map/dot_general | solution.py:43
  358.5 0.0 reduce-scatter.4.cloned.1.call-update
  358.5 0.2 reduce-scatter.8.cloned.1.call-start
  358.7 42.6 %all-gather.9.cloned.1.call-done = bf16[1024,1792]{1,0:T(8,128)(2,1)} async-done(((bf16[64,1792]{1,0:T(8,128)(2,1)}), bf16[1024,1792]{1,0:T(8,128)(2,1)}) %all-gather.9.cloned.1.call-update) | async-done | bytes 3670032 | tf_op jit(solution)/shard_map/all_gather | solution.py:58
  401.3 6.0 %fusion.6 = f32[1024,512]{1,0:T(8,128)} fusion(bf16[1024,1792]{1,0:T(8,128)(2,1)} %all-gather.9.cloned.1.call-done, bf16[512,1792]{1,0:T(8,128)(2,1)} %param.7), kind=kOutput, calls=%fused_computation.16 | convolution fusion | flops 1879048192 | bytes 7602176 | tf_op jit(solution)/shard_map/dot_general | solution.py:8
  407.4 45.1 %all-gather.11.cloned.1.call-done = bf16[1024,1792]{1,0:T(8,128)(2,1)} async-done(((bf16[64,1792]{1,0:T(8,128)(2,1)}), bf16[1024,1792]{1,0:T(8,128)(2,1)}) %all-gather.11.cloned.1.call-update) | async-done | bytes 3670032 | tf_op jit(solution)/shard_map/all_gather | solution.py:59
  452.5 6.6 %convolution_add_fusion = f32[1024,512]{1,0:T(8,128)} fusion(f32[1024,512]{1,0:T(8,128)} %fusion.6, bf16[1024,1792]{1,0:T(8,128)(2,1)} %all-gather.11.cloned.1.call-done, bf16[512,1792]{1,0:T(8,128)(2,1)} %param.8), kind=kOutput, calls=%fused_computation.8 | convolution fusion | flops 1879572480 | bytes 9699328 | tf_op jit(solution)/shard_map/dot_general | solution.py:8
  459.1 0.0 reduce-scatter.8.cloned.1.call-update
  459.2 5.7 %convolution_convert_fusion = bf16[1792,512]{1,0:T(8,128)(2,1)} fusion(bf16[1024,1792]{1,0:T(8,128)(2,1)} %get-tuple-element.12, bf16[1024,512]{1,0:T(8,128)(2,1)} %all-gather.7.cloned.1.call-done), kind=kOutput, calls=%fused_computation.3 | convolution fusion | flops 1879965696 | bytes 6553600 | tf_op jit(solution)/shard_map/dot_general | solution.py:14
  464.8 23.3 %reduce-scatter.4.cloned.1.call-done = f32[128,512]{1,0:T(8,128)} async-done(((f32[1024,512]{1,0:T(8,128)}), f32[128,512]{1,0:T(8,128)}) %reduce-scatter.4.cloned.1.call-update) | async-done | bytes 262160 | tf_op jit(solution)/shard_map/reduce_scatter | solution.py:42
  488.1 1.6 convert_element_type.31
  489.7 5.4 %fusion = bf16[512,1792]{0,1:T(8,128)(2,1)} fusion(bf16[1024,1792]{1,0:T(8,128)(2,1)} %all-gather.9.cloned.1.call-done, bf16[1024,512]{1,0:T(8,128)(2,1)S(1)} %copy-done.2), kind=kOutput, calls=%fused_computation.6 | convolution fusion | flops 1879965696 | bytes 6553600 | tf_op jit(solution)/shard_map/dot_general | solution.py:14
  495.1 3.8 copy.10
  498.9 5.4 %fusion.1 = bf16[512,1792]{0,1:T(8,128)(2,1)} fusion(bf16[1024,1792]{1,0:T(8,128)(2,1)} %all-gather.11.cloned.1.call-done, bf16[1024,512]{1,0:T(8,128)(2,1)S(1)} %copy-done.2), kind=kOutput, calls=%fused_computation.7 | convolution fusion | flops 1879965696 | bytes 6553600 | tf_op jit(solution)/shard_map/dot_general | solution.py:14
  504.3 3.8 copy.11
  508.1 15.2 %reduce-scatter.8.cloned.1.call-done = f32[128,512]{1,0:T(8,128)} async-done(((f32[1024,512]{1,0:T(8,128)}), f32[128,512]{1,0:T(8,128)}) %reduce-scatter.8.cloned.1.call-update) | async-done | bytes 262160 | tf_op jit(solution)/shard_map/reduce_scatter | solution.py:61
  523.3 1.6 convert_element_type.34
Async XLA Ops:
  7.2 53.6 %copy-start = (bf16[1792,512]{1,0:T(8,128)(2,1)S(1)}, bf16[1792,512]{1,0:T(8,128)(2,1)}, u32[]{:S(2)}) copy-start(bf16[1792,512]{1,0:T(8,128)(2,1)} %param.9) | copy-start | bytes 5505028
  7.2 28.5 %all-gather.5.cloned.1.call-start = ((), (), s32[]{:S(2)}) async-start(), calls=%async_computation.3 | async-start | bytes 1179648 | tf_op jit(solution)/shard_map/all_gather | solution.py:20
  7.9 52.9 %all-gather.7.cloned.1.call-start = ((), (), s32[]{:S(2)}) async-start(), calls=%async_computation.6 | async-start | bytes 1179648 | tf_op jit(solution)/shard_map/all_gather | solution.py:48
  8.7 254.4 %all-reduce.2.cloned.1.call-start = ((), (), s32[]{:S(2)}) async-start(), calls=%async_computation.4 | async-start | bytes 29360128 | tf_op jit(solution)/shard_map/psum | solution.py:30
  35.7 4.0 copy-start.1
  35.7 4.0 copy-start.2
  47.7 302.2 %reduce-scatter.6.cloned.1.call-start = ((), (), s32[]{:S(2)}) async-start(), calls=%async_computation.7 | async-start | bytes 7798784 | tf_op jit(solution)/shard_map/reduce_scatter | solution.py:50
  67.1 334.2 %all-gather.9.cloned.1.call-start = ((), (), s32[]{:S(2)}) async-start(), calls=%async_computation.8 | async-start | bytes 3899392 | tf_op jit(solution)/shard_map/all_gather | solution.py:58
  352.4 100.1 %all-gather.11.cloned.1.call-start = ((), (), s32[]{:S(2)}) async-start(), calls=%async_computation.9 | async-start | bytes 3899392 | tf_op jit(solution)/shard_map/all_gather | solution.py:59
  353.0 135.2 %reduce-scatter.4.cloned.1.call-start = ((), (), s32[]{:S(2)}) async-start(), calls=%async_computation.5 | async-start | bytes 2359296 | tf_op jit(solution)/shard_map/reduce_scatter | solution.py:42
  358.5 164.8 %reduce-scatter.8.cloned.1.call-start = ((), (), s32[]{:S(2)}) async-start(), calls=%async_computation.10 | async-start | bytes 2359296 | tf_op jit(solution)/shard_map/reduce_scatter | solution.py:61
Sparse Core Ops, SparseCore 0:
  9.7 25.9 all-gather.4
  37.4 23.3 all-gather.6
  64.4 198.5 all-reduce.1
  266.4 83.4 reduce-scatter.5
  352.5 48.7 all-gather.8
  403.9 48.5 all-gather.10
  454.9 33.1 reduce-scatter.3
  490.5 32.7 reduce-scatter.7
where the time goes:
time: 532 us
  waiting for transfers between devices  436 us (82%)
  matrix products  47 us (9%)
  other arithmetic  27 us (5%)
  between operations  14.2 us (3%)
  local copies, waits for them, and re-layouts  7.63 us (1%)
    psum x1, waiting for transfers between devices, local(): joined = lax.psum(partial_sums, 'row')  196 us
    reduce_scatter x1, waiting for transfers between devices, local(): lax.psum_scatter(contract_last(rows_in, down_weight), 'row', scatter_dime...  71.4 us
    all_gather x1, waiting for transfers between devices, local(): lax.all_gather(up_grad, 'row', axis=0, tiled=True)  45.1 us
    all_gather x1, waiting for transfers between devices, local(): lax.all_gather(gate_grad, 'row', axis=0, tiled=True)  42.6 us
    all_gather x1, waiting for transfers between devices, local(): token_panel = lax.all_gather(tokens, 'col', axis=0, tiled=True)  27 us
    reduce_scatter x1, waiting for transfers between devices, local(): lax.psum_scatter(jnp.dot(rows_in, down_weight, preferred_element_type=jnp...  23.3 us
    dot_general x3, matrix products, contract_last(): lax.dot_general(left, right, (((1,), (1,)), ((), ())), preferred_element_...  19 us
    dot_general x3, matrix products, contract_first(): lax.dot_general(left, right, (((0,), (0,)), ((), ())), preferred_element_...  16.4 us
  transfers between devices with their start and end apart: 8, of which 8 were waited for; matrix products, arithmetic and copies ran while one was open for 15% of the time, Pallas kernels for 0%

commit v1 on v0

--- a/solution.py
+++ b/solution.py
@@ -2,6 +2,17 @@
 import jax.numpy as jnp
 from jax import lax
 from jax.sharding import PartitionSpec as P
+
+
+def bind_views(array_here, axis_name):
+    full_n = lax.psum(1, axis_name)
+    near = array_here
+    for to_i in [
+        [(dd, dd ^ idx) for dd in range(full_n)] for idx in (1, 2, 4, 8, 16) if idx < full_n
+    ]:
+        f_next = lax.ppermute(near, axis_name, to_i)
+        near = near + f_next
+    return near
 
 
 def contract_last(left, right):
@@ -27,7 +38,7 @@
         ],
         axis=1,
     )
-    joined = lax.psum(partial_sums, "row")
+    joined = bind_views(partial_sums, axis_name="row")
     gate_all = joined[:, :hidden_width]
     up_all = joined[:, hidden_width:]
     sigmoid_all = jax.nn.sigmoid(gate_all)

time: 532 us -> 1590 us (2.99)
  waiting for transfers between devices: 436 us -> 1440 us
  other arithmetic: 27 us -> 73.5 us
    ppermute x0 -> x4, waiting for transfers between devices: none -> 1280 us  [bind_views(): f_next = lax.ppermute(near, axis_name, to_i)]
    psum x1 -> x0, waiting for transfers between devices: 196 us -> none  [local(): joined = lax.psum(partial_sums, 'row')]
    reduce_scatter x1, waiting for transfers between devices: 71.4 us -> 0.01 us  [local(): lax.psum_scatter(contract_last(rows_in, down_weight), 'row', scatter_dime...]
    add x0 -> x4, other arithmetic: none -> 50.5 us  [bind_views(): near = near + f_next]
  transfers between devices with their start and end apart: 8 -> 11, of which waited for: 8 -> 9; matrix products, arithmetic and copies ran while one was open for 15% -> 6% of each run, Pallas kernels for 0% -> 0%
where the time goes in v1:
time: 1590 us
  waiting for transfers between devices  1440 us (91%)
  other arithmetic  73.5 us (5%)
  matrix products  46.9 us (3%)
    ppermute x4, waiting for transfers between devices, bind_views(): f_next = lax.ppermute(near, axis_name, to_i)  1280 us
    add x4, other arithmetic, bind_views(): near = near + f_next  50.5 us
    all_gather x1, waiting for transfers between devices, local(): lax.all_gather(up_grad, 'row', axis=0, tiled=True)  45.1 us
    all_gather x1, waiting for transfers between devices, local(): lax.all_gather(gate_grad, 'row', axis=0, tiled=True)  43.4 us
  transfers between devices with their start and end apart: 11, of which 9 were waited for; matrix products, arithmetic and copies ran while one was open for 6% of the time, Pallas kernels for 0%

profile of v1, /device:TPU:0, one launch (start us, length us, event | category | flops | bytes accessed | tf_op | source)
XLA Modules:
  0.0 1591.2 jit_solution(7540246657156932345)
XLA Ops:
  7.2 0.0 all-gather.5.cloned.1.call-start
  7.2 0.7 all-gather.5.cloned.1.call-update
  7.9 0.0 all-gather.7.cloned.1.call-start
  8.0 27.7 %all-gather.5.cloned.1.call-done = bf16[1024,512]{1,0:T(8,128)(2,1)} async-done(((bf16[128,512]{1,0:T(8,128)(2,1)}), bf16[1024,512]{1,0:T(8,128)(2,1)}) %all-gather.5.cloned.1.call-update) | async-done | bytes 1048592 | tf_op jit(solution)/shard_map/all_gather | solution.py:31
  35.7 4.0 fusion.3
  39.7 2.1 fusion.4
  41.8 1.9 pad_maximum_fusion
  43.8 1.0 copy-done.1
  44.8 1.5 collective-permute-start
  46.2 316.0 %collective-permute-done = f32[1024,3584]{1,0:T(8,128)} collective-permute-done((f32[1024,3584]{1,0:T(8,128)S(1)}, f32[1024,3584]{1,0:T(8,128)}, u32[]{:S(2)}, u32[]{:S(2)}) %collective-permute-start) | collective-permute-done | bytes 14680096 | tf_op jit(solution)/shard_map/ppermute | solution.py:13
  362.3 8.1 fusion.2
  370.3 3.1 collective-permute-start.1
  373.4 315.2 %collective-permute-done.1 = f32[1024,3584]{1,0:T(8,128)} collective-permute-done((f32[1024,3584]{1,0:T(8,128)S(1)}, f32[1024,3584]{1,0:T(8,128)}, u32[]{:S(2)}, u32[]{:S(2)}) %collective-permute-start.1) | collective-permute-done | bytes 14680096 | tf_op jit(solution)/shard_map/ppermute | solution.py:13
  688.6 10.9 add.34
  699.4 1.5 collective-permute-start.2
  700.9 0.0 all-gather.7.cloned.1.call-update
  701.0 0.0 reduce-scatter.6.cloned.1.call-start
  701.0 314.5 %collective-permute-done.2 = f32[1024,3584]{1,0:T(8,128)} collective-permute-done((f32[1024,3584]{1,0:T(8,128)}, f32[1024,3584]{1,0:T(8,128)}, u32[]{:S(2)}, u32[]{:S(2)}) %collective-permute-start.2) | collective-permute-done | bytes 14680096 | tf_op jit(solution)/shard_map/ppermute | solution.py:13
  1015.5 15.7 add.35
  1031.2 3.0 collective-permute-start.3
  1034.2 6.3 fusion.6
  1040.5 0.0 reduce-scatter.6.cloned.1.call-update
  1040.5 0.0 all-gather.9.cloned.1.call-start
  1040.6 336.8 %collective-permute-done.3 = f32[1024,3584]{1,0:T(8,128)} collective-permute-done((f32[1024,3584]{1,0:T(8,128)}, f32[1024,3584]{1,0:T(8,128)}, u32[]{:S(2)}, u32[]{:S(2)}) %collective-permute-start.3) | collective-permute-done | bytes 14680096 | tf_op jit(solution)/shard_map/ppermute | solution.py:13
  1377.4 15.9 add.36
  1393.2 15.3 slice_multiply_fusion
  1408.6 2.5 multiply_convert_fusion.1
  1411.0 0.0 all-gather.9.cloned.1.call-update
  1411.0 0.0 all-gather.11.cloned.1.call-start
  1411.1 0.5 all-gather.11.cloned.1.call-update
  1411.6 0.0 reduce-scatter.4.cloned.1.call-start
  1411.7 5.5 fusion.5
  1417.2 0.0 reduce-scatter.4.cloned.1.call-update
  1417.2 0.2 reduce-scatter.8.cloned.1.call-start
  1417.4 43.4 %all-gather.9.cloned.1.call-done = bf16[1024,1792]{1,0:T(8,128)(2,1)} async-done(((bf16[64,1792]{1,0:T(8,128)(2,1)}), bf16[1024,1792]{1,0:T(8,128)(2,1)}) %all-gather.9.cloned.1.call-update) | async-done | bytes 3670032 | tf_op jit(solution)/shard_map/all_gather | solution.py:69
  1460.9 6.0 fusion.7
  1466.9 45.1 %all-gather.11.cloned.1.call-done = bf16[1024,1792]{1,0:T(8,128)(2,1)} async-done(((bf16[64,1792]{1,0:T(8,128)(2,1)}), bf16[1024,1792]{1,0:T(8,128)(2,1)}) %all-gather.11.cloned.1.call-update) | async-done | bytes 3670032 | tf_op jit(solution)/shard_map/all_gather | solution.py:70
  1512.0 6.6 convolution_add_fusion
  1518.6 0.0 reduce-scatter.8.cloned.1.call-update
  1518.6 5.7 convolution_convert_fusion
  1524.3 23.2 %reduce-scatter.4.cloned.1.call-done = f32[128,512]{1,0:T(8,128)} async-done(((f32[1024,512]{1,0:T(8,128)}), f32[128,512]{1,0:T(8,128)}) %reduce-scatter.4.cloned.1.call-update) | async-done | bytes 262160 | tf_op jit(solution)/shard_map/reduce_scatter | solution.py:53
  1547.5 1.6 convert_element_type.31
  1549.1 5.4 fusion
  1554.5 3.8 copy.10
  1558.3 5.4 fusion.1
  1563.7 3.8 copy.11
  1567.5 15.2 reduce-scatter.8.cloned.1.call-done
  1582.7 1.6 convert_element_type.34
  (9 shorter events, 0.0 us)
Async XLA Ops:
  7.2 1027.1 %copy-start = (bf16[1792,512]{1,0:T(8,128)(2,1)S(1)}, bf16[1792,512]{1,0:T(8,128)(2,1)}, u32[]{:S(2)}) copy-start(bf16[1792,512]{1,0:T(8,128)(2,1)} %param.9) | copy-start | bytes 5505028
  7.2 28.5 %all-gather.5.cloned.1.call-start = ((), (), s32[]{:S(2)}) async-start(), calls=%async_computation.3 | async-start | bytes 1179648 | tf_op jit(solution)/shard_map/all_gather | solution.py:31
  7.9 1026.3 %all-gather.7.cloned.1.call-start = ((), (), s32[]{:S(2)}) async-start(), calls=%async_computation.5 | async-start | bytes 1179648 | tf_op jit(solution)/shard_map/all_gather | solution.py:59
  35.7 4.0 copy-start.2
  35.7 4.0 copy-start.3
  41.8 2.9 copy-start.1
  44.8 317.5 %collective-permute-start = (f32[1024,3584]{1,0:T(8,128)S(1)}, f32[1024,3584]{1,0:T(8,128)}, u32[]{:S(2)}, u32[]{:S(2)}) collective-permute-start(f32[1024,3584]{1,0:T(8,128)S(1)} %pad_maximum_fusion), channel_id=1, source_target_pairs={{0,8},{8,0},{16,24},{24,16},{32,40},{40,32},{48,56},{56,48},{64,72... | collective-permute-start | bytes 44040200 | tf_op jit(solution)/shard_map/ppermute | solution.py:13
  370.3 318.2 %collective-permute-start.1 = (f32[1024,3584]{1,0:T(8,128)S(1)}, f32[1024,3584]{1,0:T(8,128)}, u32[]{:S(2)}, u32[]{:S(2)}) collective-permute-start(f32[1024,3584]{1,0:T(8,128)S(1)} %fusion.2), channel_id=1, source_target_pairs={{0,16},{8,24},{16,0},{24,8},{32,48},{40,56},{48,32},{56,40},{64,80... | collective-permute-start | bytes 44040200 | tf_op jit(solution)/shard_map/ppermute | solution.py:13
  699.4 316.0 %collective-permute-start.2 = (f32[1024,3584]{1,0:T(8,128)}, f32[1024,3584]{1,0:T(8,128)}, u32[]{:S(2)}, u32[]{:S(2)}) collective-permute-start(f32[1024,3584]{1,0:T(8,128)} %add.34), channel_id=1, source_target_pairs={{0,32},{8,40},{16,48},{24,56},{32,0},{40,8},{48,16},{56,24},{64,96... | collective-permute-start | bytes 44040200 | tf_op jit(solution)/shard_map/ppermute | solution.py:13
  701.0 707.6 %reduce-scatter.6.cloned.1.call-start = ((), (), s32[]{:S(2)}) async-start(), calls=%async_computation.6 | async-start | bytes 7798784 | tf_op jit(solution)/shard_map/reduce_scatter | solution.py:61
  1031.2 346.2 %collective-permute-start.3 = (f32[1024,3584]{1,0:T(8,128)}, f32[1024,3584]{1,0:T(8,128)}, u32[]{:S(2)}, u32[]{:S(2)}) collective-permute-start(f32[1024,3584]{1,0:T(8,128)} %add.35), channel_id=1, source_target_pairs={{0,64},{8,72},{16,80},{24,88},{32,96},{40,104},{48,112},{56,120},{... | collective-permute-start | bytes 44040200 | tf_op jit(solution)/shard_map/ppermute | solution.py:13
  1040.5 420.3 %all-gather.9.cloned.1.call-start = ((), (), s32[]{:S(2)}) async-start(), calls=%async_computation.7 | async-start | bytes 3899392 | tf_op jit(solution)/shard_map/all_gather | solution.py:69
  1411.0 101.0 %all-gather.11.cloned.1.call-start = ((), (), s32[]{:S(2)}) async-start(), calls=%async_computation.8 | async-start | bytes 3899392 | tf_op jit(solution)/shard_map/all_gather | solution.py:70
  1411.6 135.9 %reduce-scatter.4.cloned.1.call-start = ((), (), s32[]{:S(2)}) async-start(), calls=%async_computation.4 | async-start | bytes 2359296 | tf_op jit(solution)/shard_map/reduce_scatter | solution.py:53
  1417.2 165.5 %reduce-scatter.8.cloned.1.call-start = ((), (), s32[]{:S(2)}) async-start(), calls=%async_computation.9 | async-start | bytes 2359296 | tf_op jit(solution)/shard_map/reduce_scatter | solution.py:72
Sparse Core Ops, SparseCore 0:
  9.7 25.9 all-gather.4
  701.1 23.0 all-gather.6
  1040.6 360.5 reduce-scatter.5
  1411.2 49.6 all-gather.8
  1463.4 48.5 all-gather.10
  1514.3 33.1 reduce-scatter.3
  1549.9 32.7 reduce-scatter.7
